TPU v7x, 256 devices: a whole 4x4x8 slice. The times are simulated.
256 devices in a mesh: tok: 64 (over z, x, core), head: 4 (over y).
Axes of the slice: x: 4, y: 4, z: 8, core: 2. Of those that a mesh axis runs over, the one named last changes fastest.
Arguments:
- single: bfloat16 [2048, 768], P('tok'), may hold values from -6 to 6
- pair: bfloat16 [2048, 2048, 128], P('tok', 'head'), may hold values from -161 to 161
- atoms: bfloat16 [49152, 128], P('tok'), may hold values from -60 to 60
- atom_counts: int32 [2048], P('tok'), may hold values from 4 to 24, as said below
- w_atom: bfloat16 [128, 3, 128], P(None, None, 'head'), may hold values from -0.5 to 0.5
- w_atom_token: bfloat16 [128, 768], P('head'), may hold values from -6 to 6
- ln_gain: bfloat16 [768], replicated, may hold values from 0.099609375 to 1.8984375
- w_proj: bfloat16 [768, 4, 768], P(None, None, 'head'), may hold values from -0.21875 to 0.21875
- w_pair_bias: bfloat16 [128, 16], replicated, may hold values from -3.5 to 3.5
- w_out: bfloat16 [768, 768], P('head'), may hold values from -0.21875 to 0.21875
- ln_gain2: bfloat16 [768], replicated, may hold values from 0.099609375 to 1.8984375
- w_trans: bfloat16 [768, 2, 1536], P(None, None, 'head'), may hold values from -0.21875 to 0.21875
- w_trans_out: bfloat16 [1536, 768], P('head'), may hold values from -0.15625 to 0.15625
Outputs:
- refined: bfloat16 [2048, 768], P('tok', 'head')
- atom_mix: bfloat16 [128, 49152], P('head', 'tok')
Inputs may be any that keep to these rules, and one draw needn't show every extreme that they name: `atom_counts`: every token has 4 to 24 atoms; in every draw all tokens of some group of 32 have 24 atoms.
All inputs are finite; a program needn't handle non-finite values.
Results may differ from a plain program's by a relative error of at most 0.013.
Values may be sent and summed in bfloat16 or wider, within the bound.
No kernel may reach another device: no remote copies, remote signals or barrier semaphores. Data moves between devices by JAX's collectives and lax.ppermute only.
A program may use at most 64 MiB of HBM per device.

v0:
```python
import jax
import jax.numpy as jnp
from jax import lax
from jax.sharding import PartitionSpec as P

H = 16
AH = 4
QWIN = 32
KWIN = 128
norm_eps = 1e-05
masked_value = -1000000000.0


def from_behind(block, axis, distance):
    devices = range(lax.axis_size(axis))
    route = [(i - distance, i) for i in devices if i - distance in devices]
    return lax.ppermute(block, axis, route)


def sent_to_all(value, axis):
    copies = jnp.broadcast_to(value, (lax.axis_size(axis), *value.shape))
    return lax.all_to_all(copies, axis, split_axis=0, concat_axis=0, tiled=True)


def of_everyone(value, axis):
    return sent_to_all(value, axis).astype(jnp.float32).sum(axis=0)


def joined_along(pieces, dim):
    pieces = jnp.moveaxis(pieces, 0, dim)
    dims = pieces.shape
    return pieces.reshape(*dims[:dim], dims[dim] * dims[dim + 1], *dims[dim + 2 :])


def gather_directly(value, axis, dim):
    return joined_along(sent_to_all(value, axis), dim)


def in_blocks(value, dim, size):
    before, after = (value.shape[:dim], value.shape[dim + 1 :])
    return jnp.moveaxis(value.reshape(*before, size, -1, *after), dim, 0)


def sum_at_owner(value, axis, dim):
    pieces = in_blocks(value, dim, lax.axis_size(axis))
    arrived = lax.all_to_all(pieces, axis, split_axis=0, concat_axis=0, tiled=True)
    return arrived.astype(jnp.float32).sum(axis=0)


def layer_norm(value_entries, gain):
    average = jnp.mean(value_entries, axis=-1, keepdims=True)
    centred = value_entries - average
    spread = jnp.mean(centred * centred, axis=-1, keepdims=True)
    return centred * lax.rsqrt(spread + norm_eps) * gain.astype(jnp.float32)


def atom_windows(atoms, atom_counts, w_atom):
    slot_count = atoms.shape[0]
    channels = atoms.shape[1]
    local_width = w_atom.shape[2]
    head_size = channels // AH
    local_heads = local_width // head_size
    tail_rows = (KWIN - QWIN) // 2
    head_rows = (KWIN + QWIN) // 2
    live_total = jnp.sum(atom_counts)
    device_pos = lax.axis_index("tok")
    device_last = lax.axis_size("tok") - 1
    tail_block = lax.dynamic_slice_in_dim(atoms, live_total - tail_rows, tail_rows, 0)
    previous = from_behind(tail_block, "tok", 1)
    following = from_behind(atoms[:head_rows], "tok", -1)
    extended = jnp.concatenate([atoms, jnp.zeros((head_rows, channels), atoms.dtype)], axis=0)
    extended = lax.dynamic_update_slice(extended, following, (live_total, jnp.int32(0)))
    keyed_rows = jnp.concatenate([previous, extended], axis=0)
    projected_rows = jnp.dot(
        keyed_rows, w_atom.reshape(channels, 3 * local_width), preferred_element_type=jnp.float32
    ).astype(jnp.bfloat16)
    windows = slot_count // QWIN
    queries = projected_rows[tail_rows : tail_rows + slot_count, :local_width].reshape(
        windows, QWIN, local_heads, head_size
    )
    blocked = projected_rows[:, local_width:].reshape(windows + KWIN // QWIN, QWIN, 2 * local_width)
    stacked = jnp.stack(
        [blocked[step_pos : step_pos + windows] for step_pos in range(KWIN // QWIN)], axis=1
    )
    stacked = stacked.reshape(windows, KWIN, 2, local_heads, head_size)
    key_rows = stacked[:, :, 0]
    value_rows = stacked[:, :, 1]
    scores = jnp.einsum(
        "wqhd,wkhd->whqk", queries, key_rows, preferred_element_type=jnp.float32
    ) * head_size ** (-0.5)
    window_pos = jnp.arange(windows, dtype=jnp.int32)
    key_pos = window_pos[:, None] * QWIN + jnp.arange(KWIN, dtype=jnp.int32)[None, :] - tail_rows
    key_valid = (
        (key_pos < 0) & (device_pos > 0)
        | (key_pos >= 0) & (key_pos < live_total)
        | (key_pos >= live_total) & (device_pos < device_last)
    )
    scores = jnp.where(key_valid[:, None, None, :], scores, masked_value)
    row_max = jnp.max(scores, axis=-1, keepdims=True)
    lifted = jnp.exp(scores - row_max)
    weights = (lifted / jnp.sum(lifted, axis=-1, keepdims=True)).astype(jnp.bfloat16)
    atom_out = jnp.einsum(
        "whqk,wkhd->wqhd", weights, value_rows, preferred_element_type=jnp.float32
    )
    query_live = (jnp.arange(slot_count, dtype=jnp.int32) < live_total).reshape(windows, QWIN)
    atom_out = jnp.where(query_live[:, :, None, None], atom_out, 0.0)
    return atom_out.reshape(slot_count, local_width).astype(jnp.bfloat16)


def token_means(atom_out, atom_counts):
    starts = jnp.cumsum(atom_counts) - atom_counts
    slot_position = jnp.arange(atom_out.shape[0], dtype=jnp.int32)
    member = (slot_position[None, :] >= starts[:, None]) & (
        slot_position[None, :] < (starts + atom_counts)[:, None]
    )
    totals_rows = jnp.dot(member.astype(jnp.bfloat16), atom_out, preferred_element_type=jnp.float32)
    return totals_rows / atom_counts[:, None].astype(jnp.float32)


def shards(
    single,
    pair,
    atoms,
    atom_counts,
    w_atom,
    w_atom_token,
    ln_gain,
    w_proj,
    w_pair_bias,
    w_out,
    ln_gain2,
    w_trans,
    w_trans_out,
):
    atom_out = atom_windows(atoms, atom_counts, w_atom)
    token_atoms = token_means(atom_out, atom_counts).astype(jnp.bfloat16)
    atom_part = jnp.dot(token_atoms, w_atom_token, preferred_element_type=jnp.float32)
    atom_term = of_everyone(atom_part.astype(jnp.bfloat16), "head").astype(jnp.float32)
    residual_state = single.astype(jnp.float32) + atom_term
    normed = layer_norm(residual_state, ln_gain).astype(jnp.bfloat16)
    model_width = single.shape[1]
    local_width = w_proj.shape[2]
    head_size = model_width // H
    local_heads = local_width // head_size
    row_count = normed.shape[0]
    flat_proj = w_proj.reshape(model_width, 4 * local_width)
    own_proj = jnp.dot(normed, flat_proj, preferred_element_type=jnp.float32)
    queries = own_proj[:, :local_width].astype(jnp.bfloat16)
    gate_raw = own_proj[:, 3 * local_width :]
    key_value = own_proj[:, local_width : 3 * local_width].astype(jnp.bfloat16)
    gathered = gather_directly(key_value, "tok", 0)
    token_count = gathered.shape[0]
    key_value_rows = gathered.reshape(token_count, 2, local_heads, head_size)
    pair_term = jnp.einsum(
        "ikc,ch->hik", pair, w_pair_bias, preferred_element_type=jnp.float32
    ).astype(jnp.bfloat16)
    pair_term = lax.all_to_all(pair_term, "head", split_axis=0, concat_axis=2, tiled=True)
    query_rows = queries.reshape(row_count, local_heads, head_size)
    scores = jnp.einsum(
        "qhd,khd->hqk", query_rows, key_value_rows[:, 0], preferred_element_type=jnp.float32
    ) * head_size ** (-0.5)
    scores = scores + pair_term.astype(jnp.float32)
    row_max = jnp.max(scores, axis=-1, keepdims=True)
    lifted = jnp.exp(scores - row_max)
    weights = (lifted / jnp.sum(lifted, axis=-1, keepdims=True)).astype(jnp.bfloat16)
    context = jnp.einsum(
        "hqk,khd->qhd", weights, key_value_rows[:, 1], preferred_element_type=jnp.float32
    )
    context = context.reshape(row_count, local_width)
    gated_rows = (context * jax.nn.sigmoid(gate_raw)).astype(jnp.bfloat16)
    mixing = jnp.dot(gated_rows, w_out, preferred_element_type=jnp.float32)
    quarter = model_width // lax.axis_size("head")
    offset = lax.axis_index("head") * quarter
    state_after = residual_state + of_everyone(mixing.astype(jnp.bfloat16), "head").astype(
        jnp.float32
    )
    own_share = lax.dynamic_slice_in_dim(state_after, offset, quarter, 1)
    normed_after = layer_norm(state_after, ln_gain2).astype(jnp.bfloat16)
    hidden_local = w_trans.shape[2]
    gate_up = jnp.dot(
        normed_after,
        w_trans.reshape(model_width, 2 * hidden_local),
        preferred_element_type=jnp.float32,
    )
    hidden = (jax.nn.silu(gate_up[:, :hidden_local]) * gate_up[:, hidden_local:]).astype(
        jnp.bfloat16
    )
    update = sum_at_owner(
        jnp.dot(hidden, w_trans_out, preferred_element_type=jnp.float32).astype(jnp.bfloat16),
        "head",
        1,
    )
    refined = (own_share + update).astype(jnp.bfloat16)
    return (refined, atom_out.T)


def solution(mesh):
    return jax.shard_map(
        shards,
        mesh=mesh,
        in_specs=(
            P("tok", None),
            P("tok", "head", None),
            P("tok", None),
            P("tok"),
            P(None, None, "head"),
            P("head", None),
            P(),
            P(None, None, "head"),
            P(),
            P("head", None),
            P(),
            P(None, None, "head"),
            P("head", None),
        ),
        out_specs=(P("tok", "head"), P("head", "tok")),
        check_vma=False,
    )
```

profile of v0, /device:TPU:2, one launch (start us, length us, event | category | flops | bytes accessed | tf_op | source)
XLA Modules:
  0.0 143.4 jit_solution(10837507547731607174)
XLA Ops:
  1.6 1.9 %fusion.67 = (f32[32]{0:T(128)S(1)}, s32[32]{0:T(128)}, s32[]{:T(128)}) fusion(s32[32]{0:T(128)} %param.16, s32[32]{0:T(128)S(1)} %reduce.4), kind=kLoop, calls=%fused_computation.98 | loop fusion | flops 95 | bytes 516 | tf_op jit(solution)/shard_map/convert_element_type | solution.py:117
  5.6 1.9 %collective-permute-start = (bf16[48,128]{1,0:T(8,128)(2,1)S(1)}, bf16[48,128]{1,0:T(8,128)(2,1)S(1)}, u32[]{:S(2)}, u32[]{:S(2)}) collective-permute-start(bf16[48,128]{1,0:T(8,128)(2,1)S(1)} %constant_dynamic-slice_fusion), channel_id=1, source_target_pairs={{0,4},{4,8},{8,12},{12,16},{16,20},{20,24},{24,28},{28,32},{32,36}... | collective-permute-start | bytes 36872 | tf_op jit(solution)/shard_map/ppermute | solution.py:17
  8.2 3.6 %collective-permute-start.1 = (bf16[80,128]{1,0:T(8,128)(2,1)S(1)}, bf16[80,128]{1,0:T(8,128)(2,1)S(1)}, u32[]{:S(2)}, u32[]{:S(2)}) collective-permute-start(bf16[80,128]{1,0:T(8,128)(2,1)S(1)} %slice.56), channel_id=1, source_target_pairs={{4,0},{8,4},{12,8},{16,12},{20,16},{24,20},{28,24},{32,28},{36,32}... | collective-permute-start | bytes 61448 | tf_op jit(solution)/shard_map/ppermute | solution.py:17
  21.7 1.4 fusion.10
  24.4 4.5 %all-to-all-start = ((bf16[4,32,768]{2,1,0:T(8,128)(2,1)}), bf16[4,32,768]{2,1,0:T(8,128)(2,1)S(1)}, u32[]{:S(2)}, u32[]{:S(2)}) async-start(bf16[4,32,768]{2,1,0:T(8,128)(2,1)} %broadcast_in_dim.34), calls=%async_computation | async-start | bytes 393216 | tf_op jit(solution)/shard_map/all_to_all | solution.py:22
  28.9 3.4 %convolution_convert_fusion = bf16[16,32,512]{2,0,1:T(8,128)(2,1)S(1)} fusion(bf16[32,512,128]{2,1,0:T(8,128)(2,1)} %param.14, bf16[128,16]{0,1:T(8,128)(2,1)S(1)} %copy-done.8), kind=kOutput, calls=%fused_computation.6 | convolution fusion | flops 67371008 | bytes 4722688 | tf_op jit(solution)/shard_map/ikc,ch->hik/dot_general | solution.py:154
  33.4 1.8 %all-to-all-done = bf16[4,32,768]{2,1,0:T(8,128)(2,1)S(1)} async-done(((bf16[4,32,768]{2,1,0:T(8,128)(2,1)}), bf16[4,32,768]{2,1,0:T(8,128)(2,1)S(1)}, u32[]{:S(2)}, u32[]{:S(2)}) %all-to-all-start) | async-done | bytes 196640 | tf_op jit(solution)/shard_map/all_to_all | solution.py:22
  35.2 3.5 %all-to-all-start.2 = ((bf16[16,32,512]{2,1,0:T(8,128)(2,1)}), bf16[16,32,512]{2,1,0:T(8,128)(2,1)S(1)}, u32[]{:S(2)}, u32[]{:S(2)}) async-start(bf16[16,32,512]{2,1,0:T(8,128)(2,1)} %copy.66), calls=%async_computation.2 | async-start | bytes 1048576 | tf_op jit(solution)/shard_map/all_to_all | solution.py:157
  40.3 6.9 %all-to-all-done.2 = bf16[16,32,512]{2,1,0:T(8,128)(2,1)S(1)} async-done(((bf16[16,32,512]{2,1,0:T(8,128)(2,1)}), bf16[16,32,512]{2,1,0:T(8,128)(2,1)S(1)}, u32[]{:S(2)}, u32[]{:S(2)}) %all-to-all-start.2) | async-done | bytes 524320 | tf_op jit(solution)/shard_map/all_to_all | solution.py:157
  48.4 12.4 %all-to-all-start.1 = ((bf16[64,32,384]{2,1,0:T(8,128)(2,1)}), bf16[64,32,384]{2,1,0:T(8,128)(2,1)S(1)}, u32[]{:S(2)}, u32[]{:S(2)}) async-start(bf16[64,32,384]{2,1,0:T(8,128)(2,1)} %broadcast_in_dim.35), calls=%async_computation.1 | async-start | bytes 3145728 | tf_op jit(solution)/shard_map/all_to_all | solution.py:22
  63.0 1.4 copy.80
  64.4 2.9 %reshape.182 = f32[4,32,2048]{2,1,0:T(8,128)} reshape(f32[4,32,4,512]{3,2,1,0:T(4,128)} %bitcast.71) | data formatting | bytes 2097152 | tf_op jit(solution)/shard_map/convert_element_type | solution.py:162
  67.3 33.6 %all-to-all-done.1 = bf16[64,32,384]{2,1,0:T(8,128)(2,1)S(1)} async-done(((bf16[64,32,384]{2,1,0:T(8,128)(2,1)}), bf16[64,32,384]{2,1,0:T(8,128)(2,1)S(1)}, u32[]{:S(2)}, u32[]{:S(2)}) %all-to-all-start.1) | async-done | bytes 1572896 | tf_op jit(solution)/shard_map/all_to_all | solution.py:22
  100.9 4.7 %reshape_reshape.3 = bf16[2048,2,4,48]{3,2,1,0:T(4,128)(2,1)} reshape(bf16[64,32,384]{2,1,0:T(8,128)(2,1)S(1)} %all-to-all-done.1) | data formatting | bytes 3145728 | tf_op jit(solution)/shard_map/reshape;reshape | solution.py:153
  105.6 4.0 %fusion.65 = (bf16[2048,1,4,48]{3,2,1,0:T(4,128)(2,1)}, bf16[2048,1,4,48]{3,2,1,0:T(4,128)(2,1)S(1)}) fusion(bf16[2048,2,4,48]{3,2,1,0:T(4,128)(2,1)} %reshape_reshape.3), kind=kLoop, calls=%fused_computation.96 | loop fusion | bytes 3145728 | tf_op jit(solution)/shard_map/slice | solution.py:160
  109.6 4.0 %copy.74 = bf16[2048,1,4,48]{0,3,2,1:T(8,128)(2,1)} copy(bf16[2048,1,4,48]{3,2,1,0:T(4,128)(2,1)} %get-tuple-element.4) | data formatting | bytes 1572864
  113.6 1.7 %fusion.4 = f32[4,32,2048]{2,1,0:T(8,128)S(1)} fusion(f32[4,32,2048]{2,1,0:T(8,128)} %reshape.182, bf16[2048,1,4,48]{0,3,2,1:T(8,128)(2,1)} %copy.74, bf16[32,4,48]{2,1,0:T(4,128)(2,1)S(1)} %reshape.178), kind=kOutput, calls=%fused_computation.5 | convolution fusion | flops 25690112 | bytes 2895872 | tf_op jit(solution)/shard_map/qhd,khd->hqk/dot_general | solution.py:159
  116.7 2.3 %copy.73 = bf16[2048,1,4,48]{0,3,2,1:T(8,128)(2,1)} copy(bf16[2048,1,4,48]{3,2,1,0:T(4,128)(2,1)S(1)} %get-tuple-element.5) | data formatting | bytes 1572864
  119.1 2.2 %convolution_bitcast_fusion.1 = f32[32,4,48]{2,0,1:T(8,128)S(1)} fusion(bf16[2048,1,4,48]{0,3,2,1:T(8,128)(2,1)} %copy.73, f32[4,32]{1,0:T(4,128)S(1)} %fusion.70, f32[4,32,2048]{2,1,0:T(8,128)} %copy-done.1), kind=kOutput, calls=%fused_computation.19 | convolution fusion | flops 25954432 | bytes 1860096 | tf_op jit(solution)/shard_map/hqk,khd->qhd/dot_general | solution.py:166
  122.4 3.4 %all-to-all-start.3 = ((bf16[4,32,768]{2,1,0:T(8,128)(2,1)}), bf16[4,32,768]{2,1,0:T(8,128)(2,1)S(1)}, u32[]{:S(2)}, u32[]{:S(2)}) async-start(bf16[4,32,768]{2,1,0:T(8,128)(2,1)} %broadcast_in_dim.36), calls=%async_computation.3 | async-start | bytes 393216 | tf_op jit(solution)/shard_map/all_to_all | solution.py:22
  125.8 1.5 %copy.75 = bf16[96,8,2,384]{3,1,2,0:T(8,128)(2,1)S(1)} copy(bf16[96,8,2,384]{3,2,1,0:T(2,128)(2,1)} %bitcast.73) | data formatting | bytes 2359296
  127.3 4.8 %all-to-all-done.3 = bf16[4,32,768]{2,1,0:T(8,128)(2,1)S(1)} async-done(((bf16[4,32,768]{2,1,0:T(8,128)(2,1)}), bf16[4,32,768]{2,1,0:T(8,128)(2,1)S(1)}, u32[]{:S(2)}, u32[]{:S(2)}) %all-to-all-start.3) | async-done | bytes 196640 | tf_op jit(solution)/shard_map/all_to_all | solution.py:22
  133.8 3.3 %all-to-all-start.4 = ((bf16[4,32,192]{2,1,0:T(8,128)(2,1)}), bf16[4,32,192]{2,1,0:T(8,128)(2,1)S(1)}, u32[]{:S(2)}, u32[]{:S(2)}) async-start(bf16[4,32,192]{2,1,0:T(8,128)(2,1)} %bitcast.68), calls=%async_computation.4 | async-start | bytes 131072 | tf_op jit(solution)/shard_map/all_to_all | solution.py:46
  137.1 5.6 %all-to-all-done.4 = bf16[4,32,192]{2,1,0:T(8,128)(2,1)S(1)} async-done(((bf16[4,32,192]{2,1,0:T(8,128)(2,1)}), bf16[4,32,192]{2,1,0:T(8,128)(2,1)S(1)}, u32[]{:S(2)}, u32[]{:S(2)}) %all-to-all-start.4) | async-done | bytes 49184 | tf_op jit(solution)/shard_map/all_to_all | solution.py:46
  (84 shorter events, 22.4 us)
Async XLA Ops:
  0.6 38.4 %copy-start = (bf16[768,4,192]{0,2,1:T(8,128)(2,1)S(1)}, bf16[768,4,192]{0,2,1:T(8,128)(2,1)}, u32[]{:S(2)}) copy-start(bf16[768,4,192]{0,2,1:T(8,128)(2,1)} %param.20) | copy-start | bytes 3538948
  5.6 10.9 %collective-permute-start = (bf16[48,128]{1,0:T(8,128)(2,1)S(1)}, bf16[48,128]{1,0:T(8,128)(2,1)S(1)}, u32[]{:S(2)}, u32[]{:S(2)}) collective-permute-start(bf16[48,128]{1,0:T(8,128)(2,1)S(1)} %constant_dynamic-slice_fusion), channel_id=1, source_target_pairs={{0,4},{4,8},{8,12},{12,16},{16,20},{20,24},{24,28},{28,32},{32,36}... | collective-permute-start | bytes 36872 | tf_op jit(solution)/shard_map/ppermute | solution.py:17
  8.2 7.9 %collective-permute-start.1 = (bf16[80,128]{1,0:T(8,128)(2,1)S(1)}, bf16[80,128]{1,0:T(8,128)(2,1)S(1)}, u32[]{:S(2)}, u32[]{:S(2)}) collective-permute-start(bf16[80,128]{1,0:T(8,128)(2,1)S(1)} %slice.56), channel_id=1, source_target_pairs={{4,0},{8,4},{12,8},{16,12},{20,16},{24,20},{28,24},{32,28},{36,32}... | collective-permute-start | bytes 61448 | tf_op jit(solution)/shard_map/ppermute | solution.py:17
  20.2 0.8 copy-start.5
  21.4 2.0 %copy-start.11 = (s32[32]{0:T(128)S(1)}, s32[32]{0:T(128)}, u32[]{:S(2)}) copy-start(s32[32]{0:T(128)} %get-tuple-element.11) | copy-start | bytes 388
  21.4 2.0 %copy-start.12 = (bf16[32,768]{1,0:T(8,128)(2,1)S(1)}, bf16[32,768]{1,0:T(8,128)(2,1)}, u32[]{:S(2)}) copy-start(bf16[32,768]{1,0:T(8,128)(2,1)} %param.18) | copy-start | bytes 147460
  21.7 7.2 %copy-start.8 = (bf16[128,16]{0,1:T(8,128)(2,1)S(1)}, bf16[128,16]{0,1:T(8,128)(2,1)}, u32[]{:S(2)}) copy-start(bf16[128,16]{0,1:T(8,128)(2,1)} %param.21) | copy-start | bytes 12292
  23.3 8.9 %copy-start.7 = (bf16[768,32]{0,1:T(8,128)(2,1)}, bf16[768,32]{0,1:T(8,128)(2,1)S(1)}, u32[]{:S(2)}) copy-start(bf16[768,32]{0,1:T(8,128)(2,1)S(1)} %convert_element_type.91) | copy-start | bytes 147460
  24.4 10.8 %all-to-all-start = ((bf16[4,32,768]{2,1,0:T(8,128)(2,1)}), bf16[4,32,768]{2,1,0:T(8,128)(2,1)S(1)}, u32[]{:S(2)}, u32[]{:S(2)}) async-start(bf16[4,32,768]{2,1,0:T(8,128)(2,1)} %broadcast_in_dim.34), calls=%async_computation | async-start | bytes 393216 | tf_op jit(solution)/shard_map/all_to_all | solution.py:22
  28.9 3.4 %copy-start.9 = (bf16[768]{0:T(1024)(128)(2,1)S(1)}, bf16[768]{0:T(1024)(128)(2,1)}, u32[]{:S(2)}) copy-start(bf16[768]{0:T(1024)(128)(2,1)} %param.19) | copy-start | bytes 4612
  32.3 6.4 %copy-start.2 = (bf16[32,768]{1,0:T(8,128)(2,1)S(1)}, bf16[32,768]{1,0:T(8,128)(2,1)}, u32[]{:S(2)}) copy-start(bf16[32,768]{1,0:T(8,128)(2,1)} %param.13) | copy-start | bytes 147460
  35.2 12.0 %all-to-all-start.2 = ((bf16[16,32,512]{2,1,0:T(8,128)(2,1)}), bf16[16,32,512]{2,1,0:T(8,128)(2,1)S(1)}, u32[]{:S(2)}, u32[]{:S(2)}) async-start(bf16[16,32,512]{2,1,0:T(8,128)(2,1)} %copy.66), calls=%async_computation.2 | async-start | bytes 1048576 | tf_op jit(solution)/shard_map/all_to_all | solution.py:157
  39.5 0.6 copy-start.6
  48.4 52.5 %all-to-all-start.1 = ((bf16[64,32,384]{2,1,0:T(8,128)(2,1)}), bf16[64,32,384]{2,1,0:T(8,128)(2,1)S(1)}, u32[]{:S(2)}, u32[]{:S(2)}) async-start(bf16[64,32,384]{2,1,0:T(8,128)(2,1)} %broadcast_in_dim.35), calls=%async_computation.1 | async-start | bytes 3145728 | tf_op jit(solution)/shard_map/all_to_all | solution.py:22
  115.4 1.0 copy-start.1
  119.1 2.4 %copy-start.4 = (bf16[192,768]{1,0:T(8,128)(2,1)S(1)}, bf16[192,768]{1,0:T(8,128)(2,1)}, u32[]{:S(2)}) copy-start(bf16[192,768]{1,0:T(8,128)(2,1)} %param.22) | copy-start | bytes 884740
  121.7 5.6 %copy-start.10 = (bf16[768]{0:T(1024)(128)(2,1)S(1)}, bf16[768]{0:T(1024)(128)(2,1)}, u32[]{:S(2)}) copy-start(bf16[768]{0:T(1024)(128)(2,1)} %param.23) | copy-start | bytes 4612
  122.4 9.7 %all-to-all-start.3 = ((bf16[4,32,768]{2,1,0:T(8,128)(2,1)}), bf16[4,32,768]{2,1,0:T(8,128)(2,1)S(1)}, u32[]{:S(2)}, u32[]{:S(2)}) async-start(bf16[4,32,768]{2,1,0:T(8,128)(2,1)} %broadcast_in_dim.36), calls=%async_computation.3 | async-start | bytes 393216 | tf_op jit(solution)/shard_map/all_to_all | solution.py:22
  127.3 5.5 %copy-start.3 = (bf16[384,768]{1,0:T(8,128)(2,1)S(1)}, bf16[384,768]{1,0:T(8,128)(2,1)}, u32[]{:S(2)}) copy-start(bf16[384,768]{1,0:T(8,128)(2,1)} %param.25) | copy-start | bytes 1769476
  133.8 8.9 %all-to-all-start.4 = ((bf16[4,32,192]{2,1,0:T(8,128)(2,1)}), bf16[4,32,192]{2,1,0:T(8,128)(2,1)S(1)}, u32[]{:S(2)}, u32[]{:S(2)}) async-start(bf16[4,32,192]{2,1,0:T(8,128)(2,1)} %bitcast.68), calls=%async_computation.4 | async-start | bytes 131072 | tf_op jit(solution)/shard_map/all_to_all | solution.py:46
where the time goes:
time: 145 us; the launch traced here: 143 us
  waiting for transfers between devices  52.6 us (36%)
  local copies, waits for them, and re-layouts  36.7 us (25%)
  starting transfers between devices  32.6 us (22%)
  matrix products  11.5 us (8%)
  other arithmetic  5.67 us (4%)
  between operations  4.3 us (3%)
    all_to_all x3, waiting for transfers between devices, sent_to_all(): return lax.all_to_all(copies, axis, split_axis=0, concat_axis=0, tiled=True)  40.1 us
    all_to_all x3, starting transfers between devices, sent_to_all(): return lax.all_to_all(copies, axis, split_axis=0, concat_axis=0, tiled=True)  20.3 us
    unnamed x29, local copies, waits for them, and re-layouts  9.59 us
    all_to_all x1, waiting for transfers between devices, shards(): lax.all_to_all(pair_term, 'head', split_axis=0, concat_axis=2, tiled=True)  6.9 us
    all_to_all x1, waiting for transfers between devices, sum_at_owner(): lax.all_to_all(pieces, axis, split_axis=0, concat_axis=0, tiled=True)  5.58 us
    ppermute x2, starting transfers between devices, from_behind(): return lax.ppermute(block, axis, route)  5.54 us
    another operation x1, local copies, waits for them, and re-layouts, shards(): key_value_rows = gathered.reshape(token_count, 2, local_heads, head_size)  4.66 us
    convert_element_type x2, local copies, waits for them, and re-layouts, shards(): scores = scores + pair_term.astype(jnp.float32)  4.32 us
  transfers between devices with their start and end apart: 7, of which 5 were waited for; matrix products, arithmetic and copies ran while one was open for 12% of the time, Pallas kernels for 0%

commit v1 on v0

--- a/solution.py
+++ b/solution.py
@@ -2,6 +2,7 @@
 import jax.numpy as jnp
 from jax import lax
 from jax.sharding import PartitionSpec as P
+from jax.lax import all_to_all, psum
 
 H = 16
 AH = 4
@@ -154,7 +155,9 @@
     pair_term = jnp.einsum(
         "ikc,ch->hik", pair, w_pair_bias, preferred_element_type=jnp.float32
     ).astype(jnp.bfloat16)
-    pair_term = lax.all_to_all(pair_term, "head", split_axis=0, concat_axis=2, tiled=True)
+    pair_term = jnp.concatenate(
+        all_to_all(jnp.stack(jnp.split(pair_term, psum(1, "head"), 0), 0), "head", 0, 0), 2
+    )
     query_rows = queries.reshape(row_count, local_heads, head_size)
     scores = jnp.einsum(
         "qhd,khd->hqk", query_rows, key_value_rows[:, 0], preferred_element_type=jnp.float32

time: 145 us -> 147 us (1.014)
  waiting for transfers between devices: 52.6 us -> 55.1 us
  local copies, waits for them, and re-layouts: 36.7 us -> 35.1 us
    all_to_all x3, waiting for transfers between devices: 40.1 us -> 42.8 us  [sent_to_all(): return lax.all_to_all(copies, axis, split_axis=0, concat_axis=0, tiled=True)]
    unnamed x29 -> x33, local copies, waits for them, and re-layouts: 9.59 us -> 9.58 us
where the time goes in v1:
time: 147 us; the launch traced here: 146 us
  waiting for transfers between devices  55.1 us (37%)
  local copies, waits for them, and re-layouts  35.1 us (24%)
  starting transfers between devices  32.7 us (22%)
  matrix products  11.6 us (8%)
  other arithmetic  7.07 us (5%)
  between operations  4.34 us (3%)
    all_to_all x3, waiting for transfers between devices, sent_to_all(): return lax.all_to_all(copies, axis, split_axis=0, concat_axis=0, tiled=True)  42.8 us
    all_to_all x3, starting transfers between devices, sent_to_all(): return lax.all_to_all(copies, axis, split_axis=0, concat_axis=0, tiled=True)  20.4 us
    unnamed x33, local copies, waits for them, and re-layouts  9.58 us
    all_to_all x1, waiting for transfers between devices, shards(): all_to_all(jnp.stack(jnp.split(pair_term, psum(1, 'head'), 0), 0), 'head'...  6.75 us
    all_to_all x1, waiting for transfers between devices, sum_at_owner(): lax.all_to_all(pieces, axis, split_axis=0, concat_axis=0, tiled=True)  5.58 us
    ppermute x2, starting transfers between devices, from_behind(): return lax.ppermute(block, axis, route)  5.54 us
    another operation x1, local copies, waits for them, and re-layouts, shards(): key_value_rows = gathered.reshape(token_count, 2, local_heads, head_size)  4.66 us
    convert_element_type x2, local copies, waits for them, and re-layouts, shards(): scores = scores + pair_term.astype(jnp.float32)  4.59 us
  transfers between devices with their start and end apart: 7, of which 5 were waited for; matrix products, arithmetic and copies ran while one was open for 12% of the time, Pallas kernels for 0%

profile of v1, /device:TPU:2, one launch (start us, length us, event | category | flops | bytes accessed | tf_op | source)
XLA Modules:
  0.0 146.0 jit_solution(17943218632257808581)
XLA Ops:
  1.6 1.9 %fusion.67 = (f32[32]{0:T(128)S(1)}, s32[32]{0:T(128)}, s32[]{:T(128)}) fusion(s32[32]{0:T(128)} %param.16, s32[32]{0:T(128)S(1)} %reduce.4), kind=kLoop, calls=%fused_computation.103 | loop fusion | flops 95 | bytes 516 | tf_op jit(solution)/shard_map/convert_element_type | solution.py:118
  5.6 1.9 %collective-permute-start = (bf16[48,128]{1,0:T(8,128)(2,1)S(1)}, bf16[48,128]{1,0:T(8,128)(2,1)S(1)}, u32[]{:S(2)}, u32[]{:S(2)}) collective-permute-start(bf16[48,128]{1,0:T(8,128)(2,1)S(1)} %constant_dynamic-slice_fusion), channel_id=1, source_target_pairs={{0,4},{4,8},{8,12},{12,16},{16,20},{20,24},{24,28},{28,32},{32,36}... | collective-permute-start | bytes 36872 | tf_op jit(solution)/shard_map/ppermute | solution.py:18
  8.2 3.6 %collective-permute-start.1 = (bf16[80,128]{1,0:T(8,128)(2,1)S(1)}, bf16[80,128]{1,0:T(8,128)(2,1)S(1)}, u32[]{:S(2)}, u32[]{:S(2)}) collective-permute-start(bf16[80,128]{1,0:T(8,128)(2,1)S(1)} %slice.56), channel_id=1, source_target_pairs={{4,0},{8,4},{12,8},{16,12},{20,16},{24,20},{28,24},{32,28},{36,32}... | collective-permute-start | bytes 61448 | tf_op jit(solution)/shard_map/ppermute | solution.py:18
  11.9 4.2 %convolution_convert_fusion = bf16[16,32,512]{2,0,1:T(8,128)(2,1)} fusion(bf16[32,512,128]{2,1,0:T(8,128)(2,1)} %param.14, bf16[128,16]{0,1:T(8,128)(2,1)} %param.21), kind=kOutput, calls=%fused_computation.6 | convolution fusion | flops 67371008 | bytes 4722688 | tf_op jit(solution)/shard_map/ikc,ch->hik/dot_general | solution.py:155
  24.3 1.4 fusion.10
  27.0 4.5 %all-to-all-start = ((bf16[4,32,768]{2,1,0:T(8,128)(2,1)}), bf16[4,32,768]{2,1,0:T(8,128)(2,1)S(1)}, u32[]{:S(2)}, u32[]{:S(2)}) async-start(bf16[4,32,768]{2,1,0:T(8,128)(2,1)} %broadcast_in_dim.34), calls=%async_computation | async-start | bytes 393216 | tf_op jit(solution)/shard_map/all_to_all | solution.py:23
  33.0 4.9 %all-to-all-done = bf16[4,32,768]{2,1,0:T(8,128)(2,1)S(1)} async-done(((bf16[4,32,768]{2,1,0:T(8,128)(2,1)}), bf16[4,32,768]{2,1,0:T(8,128)(2,1)S(1)}, u32[]{:S(2)}, u32[]{:S(2)}) %all-to-all-start) | async-done | bytes 196640 | tf_op jit(solution)/shard_map/all_to_all | solution.py:23
  37.8 3.5 %all-to-all-start.2 = ((bf16[4,4,32,512]{3,1,2,0:T(4,128)(2,1)}), bf16[4,4,32,512]{3,1,2,0:T(4,128)(2,1)S(1)}, u32[]{:S(2)}, u32[]{:S(2)}) async-start(bf16[4,4,32,512]{3,1,2,0:T(4,128)(2,1)} %pad_maximum_fusion.1), calls=%async_computation.2 | async-start | bytes 1048576 | tf_op jit(solution)/shard_map/all_to_all | solution.py:159
  42.9 6.8 %all-to-all-done.2 = bf16[4,4,32,512]{3,1,2,0:T(4,128)(2,1)S(1)} async-done(((bf16[4,4,32,512]{3,1,2,0:T(4,128)(2,1)}), bf16[4,4,32,512]{3,1,2,0:T(4,128)(2,1)S(1)}, u32[]{:S(2)}, u32[]{:S(2)}) %all-to-all-start.2) | async-done | bytes 524320 | tf_op jit(solution)/shard_map/all_to_all | solution.py:159
  50.9 12.6 %all-to-all-start.1 = ((bf16[64,32,384]{2,1,0:T(8,128)(2,1)}), bf16[64,32,384]{2,1,0:T(8,128)(2,1)S(1)}, u32[]{:S(2)}, u32[]{:S(2)}) async-start(bf16[64,32,384]{2,1,0:T(8,128)(2,1)} %broadcast_in_dim.35), calls=%async_computation.1 | async-start | bytes 3145728 | tf_op jit(solution)/shard_map/all_to_all | solution.py:23
  65.8 1.6 %copy.65 = f32[4,32,4,512]{3,2,1,0:T(4,128)} copy(f32[4,32,4,512]{3,0,1,2:T(4,128)S(1)} %convert_bitcast_fusion) | data formatting | bytes 2097152 | tf_op jit(solution)/shard_map/convert_element_type | solution.py:165
  67.4 2.9 %reshape.182 = f32[4,32,2048]{2,1,0:T(8,128)} reshape(f32[4,32,4,512]{3,2,1,0:T(4,128)} %copy.65) | data formatting | bytes 2097152 | tf_op jit(solution)/shard_map/convert_element_type | solution.py:165
  70.4 33.2 %all-to-all-done.1 = bf16[64,32,384]{2,1,0:T(8,128)(2,1)S(1)} async-done(((bf16[64,32,384]{2,1,0:T(8,128)(2,1)}), bf16[64,32,384]{2,1,0:T(8,128)(2,1)S(1)}, u32[]{:S(2)}, u32[]{:S(2)}) %all-to-all-start.1) | async-done | bytes 1572896 | tf_op jit(solution)/shard_map/all_to_all | solution.py:23
  103.5 4.7 %reshape_reshape.3 = bf16[2048,2,4,48]{3,2,1,0:T(4,128)(2,1)} reshape(bf16[64,32,384]{2,1,0:T(8,128)(2,1)S(1)} %all-to-all-done.1) | data formatting | bytes 3145728 | tf_op jit(solution)/shard_map/reshape;reshape | solution.py:154
  108.2 4.0 %fusion.65 = (bf16[2048,1,4,48]{3,2,1,0:T(4,128)(2,1)}, bf16[2048,1,4,48]{3,2,1,0:T(4,128)(2,1)S(1)}) fusion(bf16[2048,2,4,48]{3,2,1,0:T(4,128)(2,1)} %reshape_reshape.3), kind=kLoop, calls=%fused_computation.101 | loop fusion | bytes 3145728 | tf_op jit(solution)/shard_map/slice | solution.py:163
  112.2 4.0 %copy.72 = bf16[2048,1,4,48]{0,3,2,1:T(8,128)(2,1)} copy(bf16[2048,1,4,48]{3,2,1,0:T(4,128)(2,1)} %get-tuple-element.4) | data formatting | bytes 1572864
  116.3 1.7 %fusion.4 = f32[4,32,2048]{2,1,0:T(8,128)S(1)} fusion(f32[4,32,2048]{2,1,0:T(8,128)} %reshape.182, bf16[2048,1,4,48]{0,3,2,1:T(8,128)(2,1)} %copy.72, bf16[32,4,48]{2,1,0:T(4,128)(2,1)S(1)} %reshape.178), kind=kOutput, calls=%fused_computation.5 | convolution fusion | flops 25690112 | bytes 2895872 | tf_op jit(solution)/shard_map/qhd,khd->hqk/dot_general | solution.py:162
  119.3 2.3 %copy.71 = bf16[2048,1,4,48]{0,3,2,1:T(8,128)(2,1)} copy(bf16[2048,1,4,48]{3,2,1,0:T(4,128)(2,1)S(1)} %get-tuple-element.5) | data formatting | bytes 1572864
  121.7 2.2 %convolution_bitcast_fusion.1 = f32[32,4,48]{2,0,1:T(8,128)S(1)} fusion(bf16[2048,1,4,48]{0,3,2,1:T(8,128)(2,1)} %copy.71, f32[4,32]{1,0:T(4,128)S(1)} %fusion.70, f32[4,32,2048]{2,1,0:T(8,128)} %copy-done.1), kind=kOutput, calls=%fused_computation.19 | convolution fusion | flops 25954432 | bytes 1860096 | tf_op jit(solution)/shard_map/hqk,khd->qhd/dot_general | solution.py:169
  125.0 3.4 %all-to-all-start.3 = ((bf16[4,32,768]{2,1,0:T(8,128)(2,1)}), bf16[4,32,768]{2,1,0:T(8,128)(2,1)S(1)}, u32[]{:S(2)}, u32[]{:S(2)}) async-start(bf16[4,32,768]{2,1,0:T(8,128)(2,1)} %broadcast_in_dim.36), calls=%async_computation.3 | async-start | bytes 393216 | tf_op jit(solution)/shard_map/all_to_all | solution.py:23
  128.4 1.5 %copy.73 = bf16[96,8,2,384]{3,1,2,0:T(8,128)(2,1)S(1)} copy(bf16[96,8,2,384]{3,2,1,0:T(2,128)(2,1)} %bitcast.76) | data formatting | bytes 2359296
  129.9 4.8 %all-to-all-done.3 = bf16[4,32,768]{2,1,0:T(8,128)(2,1)S(1)} async-done(((bf16[4,32,768]{2,1,0:T(8,128)(2,1)}), bf16[4,32,768]{2,1,0:T(8,128)(2,1)S(1)}, u32[]{:S(2)}, u32[]{:S(2)}) %all-to-all-start.3) | async-done | bytes 196640 | tf_op jit(solution)/shard_map/all_to_all | solution.py:23
  136.4 3.3 %all-to-all-start.4 = ((bf16[4,32,192]{2,1,0:T(8,128)(2,1)}), bf16[4,32,192]{2,1,0:T(8,128)(2,1)S(1)}, u32[]{:S(2)}, u32[]{:S(2)}) async-start(bf16[4,32,192]{2,1,0:T(8,128)(2,1)} %bitcast.73), calls=%async_computation.4 | async-start | bytes 131072 | tf_op jit(solution)/shard_map/all_to_all | solution.py:47
  139.7 5.6 %all-to-all-done.4 = bf16[4,32,192]{2,1,0:T(8,128)(2,1)S(1)} async-done(((bf16[4,32,192]{2,1,0:T(8,128)(2,1)}), bf16[4,32,192]{2,1,0:T(8,128)(2,1)S(1)}, u32[]{:S(2)}, u32[]{:S(2)}) %all-to-all-start.4) | async-done | bytes 49184 | tf_op jit(solution)/shard_map/all_to_all | solution.py:47
  (90 shorter events, 21.2 us)
Async XLA Ops:
  0.6 41.0 %copy-start = (bf16[768,4,192]{0,2,1:T(8,128)(2,1)S(1)}, bf16[768,4,192]{0,2,1:T(8,128)(2,1)}, u32[]{:S(2)}) copy-start(bf16[768,4,192]{0,2,1:T(8,128)(2,1)} %param.20) | copy-start | bytes 3538948
  5.6 14.2 %collective-permute-start = (bf16[48,128]{1,0:T(8,128)(2,1)S(1)}, bf16[48,128]{1,0:T(8,128)(2,1)S(1)}, u32[]{:S(2)}, u32[]{:S(2)}) collective-permute-start(bf16[48,128]{1,0:T(8,128)(2,1)S(1)} %constant_dynamic-slice_fusion), channel_id=1, source_target_pairs={{0,4},{4,8},{8,12},{12,16},{16,20},{20,24},{24,28},{28,32},{32,36}... | collective-permute-start | bytes 36872 | tf_op jit(solution)/shard_map/ppermute | solution.py:18
  8.2 11.3 %collective-permute-start.1 = (bf16[80,128]{1,0:T(8,128)(2,1)S(1)}, bf16[80,128]{1,0:T(8,128)(2,1)S(1)}, u32[]{:S(2)}, u32[]{:S(2)}) collective-permute-start(bf16[80,128]{1,0:T(8,128)(2,1)S(1)} %slice.56), channel_id=1, source_target_pairs={{4,0},{8,4},{12,8},{16,12},{20,16},{24,20},{28,24},{32,28},{36,32}... | collective-permute-start | bytes 61448 | tf_op jit(solution)/shard_map/ppermute | solution.py:18
  11.9 6.9 %copy-start.6 = (bf16[768,128]{1,0:T(8,128)(2,1)S(1)}, bf16[768,128]{1,0:T(8,128)(2,1)}, u32[]{:S(2)}) copy-start(bf16[768,128]{1,0:T(8,128)(2,1)} %param.15) | copy-start | bytes 589828
  11.9 7.9 %copy-start.14 = (bf16[128,3,32]{0,2,1:T(8,128)(2,1)S(1)}, bf16[128,3,32]{0,2,1:T(8,128)(2,1)}, u32[]{:S(2)}) copy-start(bf16[128,3,32]{0,2,1:T(8,128)(2,1)} %param.17) | copy-start | bytes 73732
  22.8 0.8 copy-start.7
  24.0 2.0 %copy-start.12 = (s32[32]{0:T(128)S(1)}, s32[32]{0:T(128)}, u32[]{:S(2)}) copy-start(s32[32]{0:T(128)} %get-tuple-element.15) | copy-start | bytes 388
  24.0 2.0 %copy-start.13 = (bf16[32,768]{1,0:T(8,128)(2,1)S(1)}, bf16[32,768]{1,0:T(8,128)(2,1)}, u32[]{:S(2)}) copy-start(bf16[32,768]{1,0:T(8,128)(2,1)} %param.18) | copy-start | bytes 147460
  24.3 7.2 %copy-start.2 = (bf16[16,32,512]{2,0,1:T(8,128)(2,1)S(1)}, bf16[16,32,512]{2,0,1:T(8,128)(2,1)}, u32[]{:S(2)}) copy-start(bf16[16,32,512]{2,0,1:T(8,128)(2,1)} %convolution_convert_fusion) | copy-start | bytes 1572868
  25.7 6.0 %copy-start.10 = (bf16[768]{0:T(1024)(128)(2,1)S(1)}, bf16[768]{0:T(1024)(128)(2,1)}, u32[]{:S(2)}) copy-start(bf16[768]{0:T(1024)(128)(2,1)} %param.19) | copy-start | bytes 4612
  26.0 1.1 copy-start.9
  27.0 10.8 %all-to-all-start = ((bf16[4,32,768]{2,1,0:T(8,128)(2,1)}), bf16[4,32,768]{2,1,0:T(8,128)(2,1)S(1)}, u32[]{:S(2)}, u32[]{:S(2)}) async-start(bf16[4,32,768]{2,1,0:T(8,128)(2,1)} %broadcast_in_dim.34), calls=%async_computation | async-start | bytes 393216 | tf_op jit(solution)/shard_map/all_to_all | solution.py:23
  31.5 9.8 %copy-start.3 = (bf16[32,768]{1,0:T(8,128)(2,1)S(1)}, bf16[32,768]{1,0:T(8,128)(2,1)}, u32[]{:S(2)}) copy-start(bf16[32,768]{1,0:T(8,128)(2,1)} %param.13) | copy-start | bytes 147460
  37.8 11.8 %all-to-all-start.2 = ((bf16[4,4,32,512]{3,1,2,0:T(4,128)(2,1)}), bf16[4,4,32,512]{3,1,2,0:T(4,128)(2,1)S(1)}, u32[]{:S(2)}, u32[]{:S(2)}) async-start(bf16[4,4,32,512]{3,1,2,0:T(4,128)(2,1)} %pad_maximum_fusion.1), calls=%async_computation.2 | async-start | bytes 1048576 | tf_op jit(solution)/shard_map/all_to_all | solution.py:159
  42.2 0.6 copy-start.8
  50.9 52.6 %all-to-all-start.1 = ((bf16[64,32,384]{2,1,0:T(8,128)(2,1)}), bf16[64,32,384]{2,1,0:T(8,128)(2,1)S(1)}, u32[]{:S(2)}, u32[]{:S(2)}) async-start(bf16[64,32,384]{2,1,0:T(8,128)(2,1)} %broadcast_in_dim.35), calls=%async_computation.1 | async-start | bytes 3145728 | tf_op jit(solution)/shard_map/all_to_all | solution.py:23
  118.0 1.0 copy-start.1
  121.7 2.4 %copy-start.5 = (bf16[192,768]{1,0:T(8,128)(2,1)S(1)}, bf16[192,768]{1,0:T(8,128)(2,1)}, u32[]{:S(2)}) copy-start(bf16[192,768]{1,0:T(8,128)(2,1)} %param.22) | copy-start | bytes 884740
  124.3 5.6 %copy-start.11 = (bf16[768]{0:T(1024)(128)(2,1)S(1)}, bf16[768]{0:T(1024)(128)(2,1)}, u32[]{:S(2)}) copy-start(bf16[768]{0:T(1024)(128)(2,1)} %param.23) | copy-start | bytes 4612
  125.0 9.7 %all-to-all-start.3 = ((bf16[4,32,768]{2,1,0:T(8,128)(2,1)}), bf16[4,32,768]{2,1,0:T(8,128)(2,1)S(1)}, u32[]{:S(2)}, u32[]{:S(2)}) async-start(bf16[4,32,768]{2,1,0:T(8,128)(2,1)} %broadcast_in_dim.36), calls=%async_computation.3 | async-start | bytes 393216 | tf_op jit(solution)/shard_map/all_to_all | solution.py:23
  129.9 5.5 %copy-start.4 = (bf16[384,768]{1,0:T(8,128)(2,1)S(1)}, bf16[384,768]{1,0:T(8,128)(2,1)}, u32[]{:S(2)}) copy-start(bf16[384,768]{1,0:T(8,128)(2,1)} %param.25) | copy-start | bytes 1769476
  136.4 8.9 %all-to-all-start.4 = ((bf16[4,32,192]{2,1,0:T(8,128)(2,1)}), bf16[4,32,192]{2,1,0:T(8,128)(2,1)S(1)}, u32[]{:S(2)}, u32[]{:S(2)}) async-start(bf16[4,32,192]{2,1,0:T(8,128)(2,1)} %bitcast.73), calls=%async_computation.4 | async-start | bytes 131072 | tf_op jit(solution)/shard_map/all_to_all | solution.py:47
